TPU v7x, 32 devices: a whole 2x2x4 slice. The times are simulated.
32 devices in a mesh: view: 4 (over y, core), bx: 2 (over x), by: 4 (over z).
Axes of the slice: x: 2, y: 2, z: 4, core: 2. Of those that a mesh axis runs over, the one named last changes fastest.
Arguments:
- estimate: float32 [2048, 512], P(('bx', 'by')), may hold values from 0.5 to 2
- recorded: float32 [4, 2048, 512], P('view', ('bx', 'by')), may hold values from 0.5 to 4
- resample: float32 [4, 4, 512, 512], P('view'), may hold values from 0 to 1, as said below
- psf_taps: float32 [4, 31], P('view'), may hold values from 0.2 to 1
- source_brick: int32 [4, 2048, 4], P('view', ('bx', 'by')), may hold values from 0 to 7, all different within a row; in each aligned block of 256 rows (0 to 255, 256 to 511, ..., all dimensions but the last counted through in order) at most 192 rows name the same one
- source_column: int32 [4, 2048, 4], P('view', ('bx', 'by')), may hold values from 0 to 255
Outputs:
- refined: float32 [2048, 512], P(('bx', 'by'))
Inputs may be any that keep to these rules, and one draw needn't show every extreme that they name: `source_brick`: in each view, the 4 bricks named for one column are different; among the columns of one brick, no joined brick is named more than 192 times, and some joined brick exactly 192 times. `resample`: all entries are nonnegative.
All inputs are finite; a program needn't handle non-finite values.
Results may differ from a plain program's by a relative error of at most 0.0001.
Values sent between devices are 32-bit elements; how exact they have to be, the bound alone decides.
A program may use at most 192 MiB of HBM per device.

v0:
```python
import jax
import jax.numpy as jnp
from jax import lax
from jax.sharding import PartitionSpec as P

ITERS = 2
precise = lax.Precision.HIGHEST


def blur_matrix(taps_row, column_len):
    spread = taps_row / jnp.sum(taps_row)
    tap_count = spread.shape[0]
    half_width = (tap_count - 1) // 2
    row_ids = lax.broadcasted_iota(jnp.int32, (column_len, column_len), 0)
    col_ids = lax.broadcasted_iota(jnp.int32, (column_len, column_len), 1)
    offset = row_ids - col_ids + half_width
    matrix = jnp.zeros((column_len, column_len), jnp.float32)
    for tap_number in range(tap_count):
        matrix = matrix + jnp.where(offset == tap_number, spread[tap_number], 0.0)
    return matrix


def per_device(estimate, recorded, resample, psf_taps, source_brick, source_column):
    bricks_x = lax.axis_size("bx")
    bricks_y = lax.axis_size("by")
    peer_count = bricks_x * bricks_y
    columns, column_len = estimate.shape
    sources = source_brick.shape[2]
    pair_count = columns * sources
    capacity = 3 * pair_count // (2 * peer_count)
    peer_ids = source_brick[0].reshape(pair_count)
    wanted = source_column[0].reshape(pair_count)
    branch_ids = lax.broadcasted_iota(jnp.int32, (columns, sources), 1).reshape(pair_count)
    peer_hits = (
        peer_ids[:, None] == lax.broadcasted_iota(jnp.int32, (pair_count, peer_count), 1)
    ).astype(jnp.int32)
    before = jnp.cumsum(peer_hits, axis=0) - peer_hits
    slot_rank = jnp.sum(before * peer_hits, axis=1)
    position = peer_ids * capacity + slot_rank
    request = (
        jnp.full((peer_count * capacity,), -1, jnp.int32)
        .at[position]
        .set(wanted * sources + branch_ids)
    )
    served = lax.all_to_all(
        request.reshape(peer_count, capacity), ("bx", "by"), split_axis=0, concat_axis=0, tiled=True
    )
    served = served.reshape(peer_count * capacity)
    owned_column = jnp.maximum(served, 0) // sources
    weights = resample[0]
    blurring = blur_matrix(psf_taps[0], column_len)
    unit_smeared = jnp.sum(blurring, axis=1)
    unit_back = jnp.einsum("b,kcb->kc", unit_smeared, weights, precision=precise)
    normalizer = None
    norm_local = None
    for sweep in range(ITERS):
        outgoing = estimate[owned_column]
        incoming = lax.all_to_all(
            outgoing.reshape(peer_count, capacity, column_len),
            ("bx", "by"),
            split_axis=0,
            concat_axis=0,
            tiled=True,
        )
        incoming = incoming.reshape(peer_count * capacity, column_len)
        pieces = incoming[position].reshape(columns, sources, column_len)
        forward = jnp.einsum("qkb,kbc->qc", pieces, weights, precision=precise)
        blurred = jnp.dot(forward, blurring, precision=precise)
        quotient = recorded[0] / blurred
        smeared = jnp.dot(quotient, blurring.T, precision=precise)
        contributions = jnp.einsum("qb,kcb->qkc", smeared, weights, precision=precise).reshape(
            pair_count, column_len
        )
        with_units = sweep == 0
        if with_units:
            unit_rows = jnp.broadcast_to(unit_back[None], (columns, sources, column_len)).reshape(
                pair_count, column_len
            )
            stacked = jnp.stack([contributions, unit_rows], axis=1)
        else:
            stacked = contributions[:, None, :]
        layers = stacked.shape[1]
        buffer = (
            jnp.zeros((peer_count * capacity, layers, column_len), jnp.float32)
            .at[position]
            .set(stacked)
        )
        returned = lax.all_to_all(
            buffer.reshape(peer_count, capacity, layers, column_len),
            ("bx", "by"),
            split_axis=0,
            concat_axis=0,
            tiled=True,
        )
        returned = returned.reshape(peer_count * capacity, layers, column_len)
        owned_sum = (
            jnp.zeros((columns, layers, column_len), jnp.float32).at[owned_column].add(returned)
        )
        correction_local = owned_sum[:, 0]
        if with_units:
            norm_local = owned_sum[:, 1]
        if sweep == 0:
            summands = jnp.stack([correction_local, norm_local])
        else:
            summands = correction_local[None]
        view_total = lax.psum(summands, "view")
        if sweep == 0:
            normalizer = view_total[1]
        estimate = estimate * (view_total[0] + 1.0) / (normalizer + 1.0)
    return estimate


def solution(mesh):
    return jax.shard_map(
        per_device,
        mesh=mesh,
        in_specs=(
            P(("bx", "by"), None),
            P("view", ("bx", "by"), None),
            P("view", None, None, None),
            P("view", None),
            P("view", ("bx", "by"), None),
            P("view", ("bx", "by"), None),
        ),
        out_specs=P(("bx", "by"), None),
        check_vma=False,
    )
```

profile of v0, /device:TPU:0, one launch (start us, length us, event | category | flops | bytes accessed | tf_op | source)
XLA Modules:
  0.0 890.5 jit_solution(9087115394177621034)
XLA Ops:
  6.5 0.9 copy.39
  7.7 0.7 broadcast_multiply_fusion.1
  8.4 2.3 reduce-window.6
  11.4 0.7 broadcast_multiply_fusion
  12.6 4.3 scatter_custom_fusion
  17.0 13.6 %all_to_all.29 = s32[8,1,192]{2,1,0:T(1,128)S(1)} all-to-all(s32[8,1,192]{2,1,0:T(1,128)S(1)} %all_to_all.18), channel_id=1, replica_groups=mesh['view'=4,'bx'=2,'by'=4] {'bx','by'}, dimensions={0} | all-to-all | bytes 12288 | tf_op jit(solution)/shard_map/all_to_all | solution.py:45
  30.8 5.0 gather_fusion
  35.7 4.6 all-to-all-start.1
  41.8 0.7 fusion.199
  42.5 0.7 fusion.198
  43.2 22.8 %fusion.58 = f32[512]{0:T(512)S(1)} fusion(f32[]{:T(128)} %bitcast.38, f32[]{:T(128)} %bitcast.37, f32[]{:T(128)} %bitcast.36, f32[]{:T(128)} %bitcast.35, f32[]{:T(128)} %bitcast.34, f32[]{:T(128)} %bitcast.33, f32[]{:T(128)} %bitcast.32, f32[]{:T(128)} %bitcast.31, f32[]{:T(128)} %bitcast.30, f32[]{:T(128)} %bitcast.29, f32[]{:T(128)} %bitcast.28, ...), kind=kLoop, calls=%fused_computation.73 | loop fusion | flops 24903168 | bytes 2172 | tf_op jit(solution)/shard_map/reduce_sum | solution.py:52
  66.0 5.7 fusion.4
  72.0 1.7 stack_reshape.7
  73.7 37.0 %all-to-all-done.1 = f32[8,192,512]{2,1,0:T(8,128)} async-done(((f32[8,192,512]{2,1,0:T(8,128)}), f32[8,192,512]{2,1,0:T(8,128)}, u32[]{:S(2)}, u32[]{:S(2)}) %all-to-all-start.1) | async-done | bytes 3145760 | tf_op jit(solution)/shard_map/all_to_all | solution.py:58
  110.7 5.9 gather_fusion.1
  116.7 1.7 reshape.214
  118.3 7.2 fusion.14
  125.6 24.4 %convolution_divide_fusion.1 = f32[256,512]{1,0:T(8,128)S(1)} fusion(f32[256,512]{1,0:T(8,128)S(1)} %fusion.14, f32[1,256,512]{2,1,0:T(8,128)S(1)} %copy-done.5, f32[]{:T(128)} %bitcast.38, f32[]{:T(128)} %bitcast.37, f32[]{:T(128)} %bitcast.36, f32[]{:T(128)} %bitcast.35, f32[]{:T(128)} %bitcast.34, f32[]{:T(128)} %bitcast.33, f32[]{:T(128)} %bitcast.32, ...), kind=kOutput, calls=%fused_computation.25 | convolution fusion | flops 830078976 | bytes 1572988 | tf_op jit(solution)/shard_map/dot_general | solution.py:68
  150.0 25.1 %convolution_bitcast_fusion.1 = f32[256,512,1]{1,0,2:T(8,128)S(1)} fusion(f32[256,512]{1,0:T(8,128)S(1)} %convolution_divide_fusion.1, f32[]{:T(128)} %bitcast.38, f32[]{:T(128)} %bitcast.37, f32[]{:T(128)} %bitcast.36, f32[]{:T(128)} %bitcast.35, f32[]{:T(128)} %bitcast.34, f32[]{:T(128)} %bitcast.33, f32[]{:T(128)} %bitcast.32, f32[]{:T(128)} %bitcast.31, ...), kind=kOutput, calls=%fused_computation.29 | convolution fusion | flops 829947904 | bytes 1048700 | tf_op jit(solution)/shard_map/dot_general | solution.py:70
  175.1 3.7 fusion.6
  178.8 1.4 copy.44
  180.2 1.8 stack_reshape.6
  182.0 2.7 pad_maximum_fusion
  184.6 5.3 copy.45
  189.9 4.3 broadcast_in_dim.160
  194.2 104.3 %scatter_fusion = f32[1536,2,512]{2,1,0:T(2,128)} fusion(f32[1536,2,512]{2,1,0:T(2,128)} %broadcast_in_dim.160, s32[1024]{0:T(1024)S(1)} %bitcast.129, f32[1024,2,512]{2,1,0:T(2,128)} %copy.45), kind=kCustom, calls=%fused_computation.5 | custom fusion | bytes 12587008 | tf_op jit(solution)/shard_map/scatter | solution.py:86
  298.5 142.2 %all_to_all.30 = f32[8,192,2,512]{3,2,1,0:T(2,128)} all-to-all(f32[8,192,2,512]{3,2,1,0:T(2,128)} %bitcast.120), channel_id=1, replica_groups=mesh['view'=4,'bx'=2,'by'=4] {'bx','by'}, dimensions={0} | all-to-all | bytes 12582912 | tf_op jit(solution)/shard_map/all_to_all | solution.py:88
  441.0 122.5 %scatter_fusion.1 = f32[256,2,512]{2,1,0:T(2,128)S(1)} fusion(f32[256,2,512]{2,1,0:T(2,128)S(1)} %broadcast_in_dim.158, s32[1536]{0:T(1024)S(1)} %fusion.67, f32[1536,2,512]{2,1,0:T(2,128)} %bitcast.121), kind=kCustom, calls=%fused_computation.6 | custom fusion | flops 1572864 | bytes 18880512 | tf_op jit(solution)/shard_map/scatter-add | solution.py:97
  563.5 0.8 slice_bitcast_fusion.1
  564.3 2.0 pad_maximum_fusion.1
  566.4 34.1 %all-reduce.3.cloned.1.call-done = f32[2,256,512]{2,0,1:T(2,128)} async-done(((f32[2,256,512]{2,0,1:T(2,128)}), f32[2,256,512]{2,0,1:T(2,128)}) %all-reduce.3.cloned.1.call-update) | async-done | bytes 1048592 | tf_op jit(solution)/shard_map/psum | solution.py:106
  600.5 2.6 slice_add_fusion
  603.1 0.8 copy-done.3
  604.1 5.0 gather_fusion.2
  609.0 76.9 %all_to_all.31 = f32[8,192,512]{2,1,0:T(8,128)} all-to-all(f32[8,192,512]{2,1,0:T(8,128)} %bitcast.124), channel_id=1, replica_groups=mesh['view'=4,'bx'=2,'by'=4] {'bx','by'}, dimensions={0} | all-to-all | bytes 6291456 | tf_op jit(solution)/shard_map/all_to_all | solution.py:58
  685.9 5.9 gather_fusion.3
  691.8 1.7 reshape.219
  693.5 7.2 fusion.19
  700.7 24.4 %convolution_divide_fusion = f32[256,512]{1,0:T(8,128)S(1)} fusion(f32[256,512]{1,0:T(8,128)S(1)} %fusion.19, f32[1,256,512]{2,1,0:T(8,128)S(1)} %copy-done.6, f32[]{:T(128)} %bitcast.38, f32[]{:T(128)} %bitcast.37, f32[]{:T(128)} %bitcast.36, f32[]{:T(128)} %bitcast.35, f32[]{:T(128)} %bitcast.34, f32[]{:T(128)} %bitcast.33, f32[]{:T(128)} %bitcast.32, ...), kind=kOutput, calls=%fused_computation.24 | convolution fusion | flops 830078976 | bytes 1572988 | tf_op jit(solution)/shard_map/dot_general | solution.py:68
  725.2 24.9 %convolution_bitcast_fusion = f32[256,512,1]{1,0,2:T(8,128)S(1)} fusion(f32[256,512]{1,0:T(8,128)S(1)} %convolution_divide_fusion, f32[]{:T(128)} %bitcast.38, f32[]{:T(128)} %bitcast.37, f32[]{:T(128)} %bitcast.36, f32[]{:T(128)} %bitcast.35, f32[]{:T(128)} %bitcast.34, f32[]{:T(128)} %bitcast.33, f32[]{:T(128)} %bitcast.32, f32[]{:T(128)} %bitcast.31, ...), kind=kOutput, calls=%fused_computation.28 | convolution fusion | flops 829947904 | bytes 1048700 | tf_op jit(solution)/shard_map/dot_general | solution.py:70
  750.1 3.7 fusion
  753.8 1.4 copy.49
  755.1 1.8 reshape.284
  756.9 7.3 scatter_custom_fusion.3
  764.2 74.6 %all_to_all.32 = f32[8,192,1,512]{3,1,2,0:T(8,128)} all-to-all(f32[8,192,1,512]{3,1,2,0:T(8,128)} %bitcast.122), channel_id=1, replica_groups=mesh['view'=4,'bx'=2,'by'=4] {'bx','by'}, dimensions={0} | all-to-all | bytes 6291456 | tf_op jit(solution)/shard_map/all_to_all | solution.py:88
  838.8 11.5 %scatter_custom_fusion.4 = f32[256,512]{1,0:T(8,128)} fusion(s32[1536]{0:T(1024)S(1)} %fusion.67, f32[1536,512]{1,0:T(8,128)} %bitcast.125, f32[]{:T(128)} %constant.37.clone.1), kind=kCustom, calls=%fused_computation.74 | custom fusion | flops 786432 | bytes 524800 | tf_op jit(solution)/shard_map/scatter-add | solution.py:97
  850.3 31.2 %all-reduce.5.cloned.1.call-done = f32[1,256,512]{2,1,0:T(8,128)} async-done(((f32[1,256,512]{2,1,0:T(8,128)}), f32[1,256,512]{2,1,0:T(8,128)}) %all-reduce.5.cloned.1.call-update) | async-done | bytes 524304 | tf_op jit(solution)/shard_map/psum | solution.py:106
  881.5 2.0 bitcast_divide_fusion
  (48 shorter events, 4.1 us)
Async XLA Ops:
  6.5 24.2 %copy-start = (f32[256,512]{1,0:T(8,128)S(1)}, f32[256,512]{1,0:T(8,128)}, u32[]{:S(2)}) copy-start(f32[256,512]{1,0:T(8,128)} %param.6) | copy-start | bytes 1572868
  35.7 4.8 copy-start.7
  35.7 75.0 %all-to-all-start.1 = ((f32[8,192,512]{2,1,0:T(8,128)}), f32[8,192,512]{2,1,0:T(8,128)}, u32[]{:S(2)}, u32[]{:S(2)}) async-start(f32[8,192,512]{2,1,0:T(8,128)} %bitcast.123), calls=%async_computation.1 | async-start | bytes 6291456 | tf_op jit(solution)/shard_map/all_to_all | solution.py:58
  40.3 560.2 %all-reduce.3.cloned.1.call-start = ((), (), s32[]{:S(2)}) async-start(), calls=%async_computation.5 | async-start | bytes 2097152 | tf_op jit(solution)/shard_map/psum | solution.py:106
  118.3 7.2 copy-start.5
  150.0 25.1 %copy-start.1 = (f32[1,4,512,512]{3,2,1,0:T(8,128)S(1)}, f32[1,4,512,512]{3,2,1,0:T(8,128)}, u32[]{:S(2)}) copy-start(f32[1,4,512,512]{3,2,1,0:T(8,128)} %param.8) | copy-start | bytes 12582916
  566.3 315.1 %all-reduce.5.cloned.1.call-start = ((), (), s32[]{:S(2)}) async-start(), calls=%async_computation.6 | async-start | bytes 1048576 | tf_op jit(solution)/shard_map/psum | solution.py:106
  603.1 0.8 copy-start.3
  693.5 7.2 copy-start.6
  725.2 24.9 %copy-start.2 = (f32[1,4,512,512]{3,2,1,0:T(8,128)S(1)}, f32[1,4,512,512]{3,2,1,0:T(8,128)}, u32[]{:S(2)}) copy-start(f32[1,4,512,512]{3,2,1,0:T(8,128)} %param.8) | copy-start | bytes 12582916
  764.2 117.3 %copy-start.4 = (f32[1,256,512]{2,0,1:T(1,128)S(1)}, f32[1,256,512]{2,0,1:T(1,128)}, u32[]{:S(2)}) copy-start(f32[1,256,512]{2,0,1:T(1,128)} %copy-done.3) | copy-start | bytes 1572868
Sparse Core Ops, SparseCore 0:
  566.4 34.0 all-reduce.2
  850.4 30.9 all-reduce.4
where the time goes:
time: 903 us; the launch traced here: 891 us
  blocking collectives  307 us (34%)
  other arithmetic  171 us (19%)
  local copies, waits for them, and re-layouts  164 us (18%)
  matrix products  126 us (14%)
  waiting for transfers between devices  102 us (11%)
  between operations  14 us (2%)
    all_to_all x2, blocking collectives, per_device(): lax.all_to_all(buffer.reshape(peer_count, capacity, layers, column_len),...  217 us
    scatter-add x2, other arithmetic, per_device(): jnp.zeros((columns, layers, column_len), jnp.float32).at[owned_column]  134 us
    scatter x2, local copies, waits for them, and re-layouts, per_device(): buffer = jnp.zeros((peer_count * capacity, layers, column_len), jnp.float...  112 us
    all_to_all x1, blocking collectives, per_device(): lax.all_to_all(outgoing.reshape(peer_count, capacity, column_len), ('bx',...  76.9 us
    psum x2, waiting for transfers between devices, per_device(): view_total = lax.psum(summands, 'view')  65.3 us
    dot_general x2, matrix products, per_device(): smeared = jnp.dot(quotient, blurring.T, precision=precise)  49.9 us
    dot_general x2, matrix products, per_device(): blurred = jnp.dot(forward, blurring, precision=precise)  48.8 us
    all_to_all x1, waiting for transfers between devices, per_device(): lax.all_to_all(outgoing.reshape(peer_count, capacity, column_len), ('bx',...  37 us
  transfers between devices with their start and end apart: 3, of which 3 were waited for; matrix products, arithmetic and copies ran while one was open for 4% of the time, Pallas kernels for 0%

commit v1 on v0

--- a/solution.py
+++ b/solution.py
@@ -103,7 +103,11 @@
             summands = jnp.stack([correction_local, norm_local])
         else:
             summands = correction_local[None]
-        view_total = lax.psum(summands, "view")
+        view_total = summands
+        for hop in (1, 2):
+            view_total = view_total + lax.ppermute(
+                view_total, "view", [(dev, dev ^ hop) for dev in range(4)]
+            )
         if sweep == 0:
             normalizer = view_total[1]
         estimate = estimate * (view_total[0] + 1.0) / (normalizer + 1.0)

time: 903 us -> 866 us (0.959)
  waiting for transfers between devices: 102 us -> 77.6 us
  between operations: 14 us -> 0.56 us
    psum x2 -> x0, waiting for transfers between devices: 65.3 us -> none  [per_device(): view_total = lax.psum(summands, 'view')]
    ppermute x0 -> x4, waiting for transfers between devices: none -> 40.3 us  [per_device(): lax.ppermute(view_total, 'view', [(dev, dev ^ hop) for dev in range(4)])]
  transfers between devices with their start and end apart: 3 -> 5, of which waited for: 3 -> 5; matrix products, arithmetic and copies ran while one was open for 4% -> 4% of each run, Pallas kernels for 0% -> 0%
where the time goes in v1:
time: 866 us; the launch traced here: 854 us
  blocking collectives  307 us (35%)
  other arithmetic  169 us (20%)
  local copies, waits for them, and re-layouts  164 us (19%)
  matrix products  126 us (15%)
  waiting for transfers between devices  77.6 us (9%)
  starting transfers between devices  8.85 us (1%)
    all_to_all x2, blocking collectives, per_device(): lax.all_to_all(buffer.reshape(peer_count, capacity, layers, column_len),...  217 us
    scatter-add x2, other arithmetic, per_device(): jnp.zeros((columns, layers, column_len), jnp.float32).at[owned_column]  133 us
    scatter x2, local copies, waits for them, and re-layouts, per_device(): buffer = jnp.zeros((peer_count * capacity, layers, column_len), jnp.float...  112 us
    all_to_all x1, blocking collectives, per_device(): lax.all_to_all(outgoing.reshape(peer_count, capacity, column_len), ('bx',...  76.3 us
    dot_general x2, matrix products, per_device(): smeared = jnp.dot(quotient, blurring.T, precision=precise)  49.6 us
    dot_general x2, matrix products, per_device(): blurred = jnp.dot(forward, blurring, precision=precise)  48.7 us
    ppermute x4, waiting for transfers between devices, per_device(): lax.ppermute(view_total, 'view', [(dev, dev ^ hop) for dev in range(4)])  40.3 us
    all_to_all x1, waiting for transfers between devices, per_device(): lax.all_to_all(outgoing.reshape(peer_count, capacity, column_len), ('bx',...  37.3 us
  transfers between devices with their start and end apart: 5, of which 5 were waited for; matrix products, arithmetic and copies ran while one was open for 4% of the time, Pallas kernels for 0%

profile of v1, /device:TPU:0, one launch (start us, length us, event | category | flops | bytes accessed | tf_op | source)
XLA Modules:
  0.0 853.9 jit_solution(4386617805516220012)
XLA Ops:
  0.0 0.9 copy.39
  1.8 2.3 reduce-window.6
  6.0 4.3 scatter_custom_fusion
  10.4 13.6 %all_to_all.29 = s32[8,1,192]{2,1,0:T(1,128)S(1)} all-to-all(s32[8,1,192]{2,1,0:T(1,128)S(1)} %all_to_all.18), channel_id=1, replica_groups=mesh['view'=4,'bx'=2,'by'=4] {'bx','by'}, dimensions={0} | all-to-all | bytes 12288 | tf_op jit(solution)/shard_map/all_to_all | solution.py:45
  24.3 5.0 gather_fusion
  29.2 5.1 all-to-all-start.1
  37.0 22.7 %fusion.58 = f32[512]{0:T(512)S(1)} fusion(f32[]{:T(128)} %bitcast.38, f32[]{:T(128)} %bitcast.37, f32[]{:T(128)} %bitcast.36, f32[]{:T(128)} %bitcast.35, f32[]{:T(128)} %bitcast.34, f32[]{:T(128)} %bitcast.33, f32[]{:T(128)} %bitcast.32, f32[]{:T(128)} %bitcast.31, f32[]{:T(128)} %bitcast.30, f32[]{:T(128)} %bitcast.29, f32[]{:T(128)} %bitcast.28, ...), kind=kLoop, calls=%fused_computation.73 | loop fusion | flops 24903168 | bytes 2172 | tf_op jit(solution)/shard_map/reduce_sum | solution.py:52
  59.7 5.7 fusion.4
  65.7 1.7 stack_reshape.7
  67.4 37.3 %all-to-all-done.1 = f32[8,192,512]{2,1,0:T(8,128)} async-done(((f32[8,192,512]{2,1,0:T(8,128)}), f32[8,192,512]{2,1,0:T(8,128)}, u32[]{:S(2)}, u32[]{:S(2)}) %all-to-all-start.1) | async-done | bytes 3145760 | tf_op jit(solution)/shard_map/all_to_all | solution.py:58
  104.7 5.9 gather_fusion.1
  110.6 1.7 reshape.214
  112.3 7.2 fusion.14
  119.6 24.3 %convolution_divide_fusion.1 = f32[256,512]{1,0:T(8,128)S(1)} fusion(f32[256,512]{1,0:T(8,128)S(1)} %fusion.14, f32[1,256,512]{2,1,0:T(8,128)S(1)} %copy-done.5, f32[]{:T(128)} %bitcast.38, f32[]{:T(128)} %bitcast.37, f32[]{:T(128)} %bitcast.36, f32[]{:T(128)} %bitcast.35, f32[]{:T(128)} %bitcast.34, f32[]{:T(128)} %bitcast.33, f32[]{:T(128)} %bitcast.32, ...), kind=kOutput, calls=%fused_computation.25 | convolution fusion | flops 830078976 | bytes 1572988 | tf_op jit(solution)/shard_map/dot_general | solution.py:68
  143.9 24.8 %convolution_bitcast_fusion.1 = f32[256,512,1]{1,0,2:T(8,128)S(1)} fusion(f32[256,512]{1,0:T(8,128)S(1)} %convolution_divide_fusion.1, f32[]{:T(128)} %bitcast.38, f32[]{:T(128)} %bitcast.37, f32[]{:T(128)} %bitcast.36, f32[]{:T(128)} %bitcast.35, f32[]{:T(128)} %bitcast.34, f32[]{:T(128)} %bitcast.33, f32[]{:T(128)} %bitcast.32, f32[]{:T(128)} %bitcast.31, ...), kind=kOutput, calls=%fused_computation.29 | convolution fusion | flops 829947904 | bytes 1048700 | tf_op jit(solution)/shard_map/dot_general | solution.py:70
  168.7 3.7 fusion.6
  172.4 1.4 copy.44
  173.8 1.8 stack_reshape.6
  175.6 2.7 pad_maximum_fusion
  178.3 5.3 copy.45
  183.5 4.3 broadcast_in_dim.160
  187.9 104.3 %scatter_fusion = f32[1536,2,512]{2,1,0:T(2,128)} fusion(f32[1536,2,512]{2,1,0:T(2,128)} %broadcast_in_dim.160, s32[1024]{0:T(1024)S(1)} %bitcast.130, f32[1024,2,512]{2,1,0:T(2,128)} %copy.45), kind=kCustom, calls=%fused_computation.5 | custom fusion | bytes 12587008 | tf_op jit(solution)/shard_map/scatter | solution.py:86
  292.2 142.2 %all_to_all.30 = f32[8,192,2,512]{3,2,1,0:T(2,128)} all-to-all(f32[8,192,2,512]{3,2,1,0:T(2,128)} %bitcast.121), channel_id=1, replica_groups=mesh['view'=4,'bx'=2,'by'=4] {'bx','by'}, dimensions={0} | all-to-all | bytes 12582912 | tf_op jit(solution)/shard_map/all_to_all | solution.py:88
  434.6 122.5 %scatter_fusion.1 = f32[256,2,512]{2,1,0:T(2,128)S(1)} fusion(f32[256,2,512]{2,1,0:T(2,128)S(1)} %broadcast_in_dim.158, s32[1536]{0:T(1024)S(1)} %fusion.67, f32[1536,2,512]{2,1,0:T(2,128)} %bitcast.122), kind=kCustom, calls=%fused_computation.6 | custom fusion | flops 1572864 | bytes 18880512 | tf_op jit(solution)/shard_map/scatter-add | solution.py:97
  558.0 0.9 pad_maximum_fusion.1
  559.0 2.6 collective-permute-done
  561.6 1.1 fusion.198
  562.8 1.9 collective-permute-start.1
  564.7 23.5 %collective-permute-done.1 = f32[2,256,512]{2,0,1:T(2,128)S(1)} collective-permute-done((f32[2,256,512]{2,0,1:T(2,128)S(1)}, f32[2,256,512]{2,0,1:T(2,128)S(1)}, u32[]{:S(2)}, u32[]{:S(2)}) %collective-permute-start.1) | collective-permute-done | bytes 1048608 | tf_op jit(solution)/shard_map/ppermute | solution.py:108
  588.1 1.3 fusion.208
  589.4 0.8 slice_add_fusion
  591.2 5.0 gather_fusion.2
  596.2 76.3 %all_to_all.31 = f32[8,192,512]{2,1,0:T(8,128)} all-to-all(f32[8,192,512]{2,1,0:T(8,128)} %bitcast.125), channel_id=1, replica_groups=mesh['view'=4,'bx'=2,'by'=4] {'bx','by'}, dimensions={0} | all-to-all | bytes 6291456 | tf_op jit(solution)/shard_map/all_to_all | solution.py:58
  672.5 5.9 gather_fusion.3
  678.4 1.7 reshape.219
  680.1 7.2 fusion.19
  687.3 24.3 %convolution_divide_fusion = f32[256,512]{1,0:T(8,128)S(1)} fusion(f32[256,512]{1,0:T(8,128)S(1)} %fusion.19, f32[1,256,512]{2,1,0:T(8,128)S(1)} %copy-done.6, f32[]{:T(128)} %bitcast.38, f32[]{:T(128)} %bitcast.37, f32[]{:T(128)} %bitcast.36, f32[]{:T(128)} %bitcast.35, f32[]{:T(128)} %bitcast.34, f32[]{:T(128)} %bitcast.33, f32[]{:T(128)} %bitcast.32, ...), kind=kOutput, calls=%fused_computation.24 | convolution fusion | flops 830078976 | bytes 1572988 | tf_op jit(solution)/shard_map/dot_general | solution.py:68
  711.7 24.8 %convolution_bitcast_fusion = f32[256,512,1]{1,0,2:T(8,128)S(1)} fusion(f32[256,512]{1,0:T(8,128)S(1)} %convolution_divide_fusion, f32[]{:T(128)} %bitcast.38, f32[]{:T(128)} %bitcast.37, f32[]{:T(128)} %bitcast.36, f32[]{:T(128)} %bitcast.35, f32[]{:T(128)} %bitcast.34, f32[]{:T(128)} %bitcast.33, f32[]{:T(128)} %bitcast.32, f32[]{:T(128)} %bitcast.31, ...), kind=kOutput, calls=%fused_computation.28 | convolution fusion | flops 829947904 | bytes 1048700 | tf_op jit(solution)/shard_map/dot_general | solution.py:70
  736.5 3.7 fusion
  740.2 1.4 copy.49
  741.5 1.8 reshape.284
  743.3 7.3 scatter_custom_fusion.3
  750.6 75.2 %all_to_all.32 = f32[8,192,1,512]{3,1,2,0:T(8,128)} all-to-all(f32[8,192,1,512]{3,1,2,0:T(8,128)} %bitcast.123), channel_id=1, replica_groups=mesh['view'=4,'bx'=2,'by'=4] {'bx','by'}, dimensions={0} | all-to-all | bytes 6291456 | tf_op jit(solution)/shard_map/all_to_all | solution.py:88
  825.7 10.8 %scatter_custom_fusion.4 = f32[256,512]{1,0:T(8,128)S(1)} fusion(s32[1536]{0:T(1024)S(1)} %fusion.67, f32[1536,512]{1,0:T(8,128)} %bitcast.126, f32[]{:T(128)} %constant.37.clone.1), kind=kCustom, calls=%fused_computation.74 | custom fusion | flops 786432 | bytes 524800 | tf_op jit(solution)/shard_map/scatter-add | solution.py:97
  836.6 1.9 collective-permute-done.2
  838.6 1.7 collective-permute-start.3
  840.4 12.3 %collective-permute-done.3 = f32[1,256,512]{2,1,0:T(8,128)S(1)} collective-permute-done((f32[1,256,512]{2,1,0:T(8,128)S(1)}, f32[1,256,512]{2,1,0:T(8,128)S(1)}, u32[]{:S(2)}, u32[]{:S(2)}) %collective-permute-start.3) | collective-permute-done | bytes 524320 | tf_op jit(solution)/shard_map/ppermute | solution.py:108
  852.7 1.0 bitcast_divide_fusion
  (53 shorter events, 8.4 us)
Async XLA Ops:
  0.0 24.2 %copy-start = (f32[256,512]{1,0:T(8,128)S(1)}, f32[256,512]{1,0:T(8,128)}, u32[]{:S(2)}) copy-start(f32[256,512]{1,0:T(8,128)} %param.6) | copy-start | bytes 1572868
  29.2 5.1 copy-start.7
  29.2 75.5 %all-to-all-start.1 = ((f32[8,192,512]{2,1,0:T(8,128)}), f32[8,192,512]{2,1,0:T(8,128)}, u32[]{:S(2)}, u32[]{:S(2)}) async-start(f32[8,192,512]{2,1,0:T(8,128)} %bitcast.124), calls=%async_computation.1 | async-start | bytes 6291456 | tf_op jit(solution)/shard_map/all_to_all | solution.py:58
  112.3 7.2 copy-start.5
  143.9 24.8 %copy-start.1 = (f32[1,4,512,512]{3,2,1,0:T(8,128)S(1)}, f32[1,4,512,512]{3,2,1,0:T(8,128)}, u32[]{:S(2)}) copy-start(f32[1,4,512,512]{3,2,1,0:T(8,128)} %param.8) | copy-start | bytes 12582916
  558.9 2.7 collective-permute-start
  562.8 25.3 %collective-permute-start.1 = (f32[2,256,512]{2,0,1:T(2,128)S(1)}, f32[2,256,512]{2,0,1:T(2,128)S(1)}, u32[]{:S(2)}, u32[]{:S(2)}) collective-permute-start(f32[2,256,512]{2,0,1:T(2,128)S(1)} %fusion.198), channel_id=1, source_target_pairs={{0,16},{8,24},{16,0},{24,8},{1,17},{9,25},{17,1},{25,9},{2,18},{10... | collective-permute-start | bytes 3145736 | tf_op jit(solution)/shard_map/ppermute | solution.py:108
  590.2 0.8 copy-start.3
  680.1 7.2 copy-start.6
  711.6 24.8 %copy-start.2 = (f32[1,4,512,512]{3,2,1,0:T(8,128)S(1)}, f32[1,4,512,512]{3,2,1,0:T(8,128)}, u32[]{:S(2)}) copy-start(f32[1,4,512,512]{3,2,1,0:T(8,128)} %param.8) | copy-start | bytes 12582916
  750.6 102.1 %copy-start.4 = (f32[1,256,512]{2,0,1:T(1,128)S(1)}, f32[1,256,512]{2,0,1:T(1,128)}, u32[]{:S(2)}) copy-start(f32[1,256,512]{2,0,1:T(1,128)} %copy-done.3) | copy-start | bytes 1572868
  836.6 2.0 collective-permute-start.2
  838.6 14.0 %collective-permute-start.3 = (f32[1,256,512]{2,1,0:T(8,128)S(1)}, f32[1,256,512]{2,1,0:T(8,128)S(1)}, u32[]{:S(2)}, u32[]{:S(2)}) collective-permute-start(f32[1,256,512]{2,1,0:T(8,128)S(1)} %bitcast_add_fusion), channel_id=1, source_target_pairs={{0,16},{8,24},{16,0},{24,8},{1,17},{9,25},{17,1},{25,9},{2,18},{10... | collective-permute-start | bytes 1572872 | tf_op jit(solution)/shard_map/ppermute | solution.py:108
